TPU v7x, 256 devices: a whole 4x4x8 slice. The times are simulated.
256 devices in a mesh: comp: 2 (over core), lat: 32 (over y, z), lon: 4 (over x).
Axes of the slice: x: 4, y: 4, z: 8, core: 2. Of those that a mesh axis runs over, the one named last changes fastest.
Arguments:
- increment: float32 [2, 8, 512, 2048], P('comp', None, 'lat', 'lon'), may hold values from -6 to 6
- diffusivity: float32 [2, 8, 512, 2048], P('comp', None, 'lat', 'lon'), may hold values from 0.03 to 0.24
- innovation: float32 [2, 8, 512, 2048], P('comp', None, 'lat', 'lon'), may hold values from -6 to 6
- land_mask: int32 [512, 2048], P('lat', 'lon'), may hold values 0 or 1
- pull_cells: int32 [2, 32, 4, 32, 1024], P('comp', 'lat', 'lon'), may hold values from 0 to 8191
- put_cells: int32 [2, 32, 4, 32, 1024], P('comp', 'lat', 'lon'), may hold values from 0 to 8191
- pull_weight: float32 [2, 32, 4, 32, 1024], P('comp', 'lat', 'lon'), may hold values from 0.2 to 0.8
- pull_count: int32 [2, 32, 4, 32], P('comp', 'lat', 'lon'), may hold values from 1 to 1024, 16384 in all within a row
Outputs:
- linear_state: float32 [2, 8, 512, 2048], P('comp', None, 'lat', 'lon')
- gradient: float32 [2, 8, 512, 2048], P('comp', None, 'lat', 'lon')
Inputs may be any that keep to these rules, and one draw needn't show every extreme that they name: `pull_count`: for each receiving block the counts over the 32 source bands add up to 16384, and the largest of them is 1024.
All inputs are finite; a program needn't handle non-finite values. No bound on the sum of `land_mask` on one device may be relied on, other than what follows from the above.
Results may differ from a plain program's by a relative error of at most 0.00002.
Values sent between devices are 32-bit elements; how exact they have to be, the bound alone decides.
No kernel may reach another device: no remote copies, remote signals or barrier semaphores. Data moves between devices by JAX's collectives and lax.ppermute only.
A program may use at most 64 MiB of HBM per device.

v0:
```python
import jax
import jax.numpy as jnp
from jax import lax
from jax.sharding import PartitionSpec as P

NSTEP = 4


def partner_2(value, axis, stride):
    mask = 2**stride
    pairs = [(source, source ^ mask) for source in range(lax.axis_size(axis))]
    return lax.ppermute(value, axis, pairs)


def extended(cells, sides, width, closed):
    for axis, dim in sides:
        count = lax.axis_size(axis)
        ends = count if closed else count - 1
        head = lax.slice_in_dim(cells, 0, width, axis=dim)
        tail = lax.slice_in_dim(cells, cells.shape[dim] - width, cells.shape[dim], axis=dim)
        cells = jnp.concatenate(
            [
                lax.ppermute(tail, axis, [(i, (i + 1) % count) for i in range(ends)]),
                cells,
                lax.ppermute(head, axis, [((i + 1) % count, i) for i in range(ends)]),
            ],
            axis=dim,
        )
    return cells


def mirrored(rows):
    partner = rows
    for bit in range(lax.axis_size("lon").bit_length() - 1):
        partner = partner_2(partner, "lon", bit)
    return partner[:, :, :, ::-1]


def at_fold():
    return (lax.axis_index("comp") == 1) & (lax.axis_index("lat") == lax.axis_size("lat") - 1)


def neighbours(field):
    lat_padded = extended(field, (("lat", 2),), 1, False)
    lon_padded = extended(field, (("lon", 3),), 1, True)
    folded = mirrored(field[:, :, -1:, :])[:, :, 0, :]
    north_edge = jnp.where(at_fold(), folded, lat_padded[:, :, -1, :])
    north = jnp.concatenate([lat_padded[:, :, 2:-1, :], north_edge[:, :, None, :]], axis=2)
    east = lon_padded[:, :, :, 2:]
    west = lon_padded[:, :, :, :-2]
    south = lat_padded[:, :, :-2, :]
    return (east, west, south, north)


def advance(field, coefficients):
    east, west, south, north = neighbours(field)
    change = coefficients[0] * (east - field) + coefficients[1] * (west - field)
    change = change + coefficients[2] * (south - field)
    change = change + coefficients[3] * (north - field)
    return field + change


def local(
    increment, diffusivity, innovation, land_mask, pull_cells, put_cells, pull_weight, pull_count
):
    height = increment.shape[2]
    width = increment.shape[3]
    cells = height * width
    bands = lax.axis_size("lat")
    ocean = lax.axis_index("comp") == 1
    mask_plane = jnp.where(
        ocean, land_mask.astype(jnp.float32), jnp.ones_like(land_mask, jnp.float32)
    )
    mask_levels = mask_plane[None, None]
    stacked = jnp.concatenate([diffusivity, mask_levels], axis=1)
    near = neighbours(stacked)
    coefficients = [
        mask_levels * side[:, -1:] * 0.5 * (diffusivity + side[:, :-1]) for side in near
    ]

    def sweep(field):
        for step in range(NSTEP):
            field = advance(field, coefficients)
        return field

    pulled = pull_cells.reshape(bands, -1)
    placed = put_cells.reshape(bands, -1)
    slot_count = pulled.shape[1]
    live = jnp.arange(slot_count, dtype=jnp.int32)[None, :] < pull_count.reshape(bands, 1)
    live_weight = jnp.where(
        live, pull_weight.reshape(bands, -1), jnp.zeros((bands, slot_count), jnp.float32)
    )
    mask_flat = mask_plane.reshape(-1)
    state = sweep(increment)
    surface = mask_flat * state[0, 0].reshape(-1)
    other_surface = partner_2(surface[None, :], "comp", 0)
    chosen = pulled
    values = jnp.take_along_axis(
        lax.all_gather(other_surface, "lat", axis=0, tiled=True), chosen, axis=1
    )
    income = jax.ops.segment_sum(
        (live_weight * values).reshape(-1), placed.reshape(-1), num_segments=cells
    )
    linear_state = state.at[0, 0].add((mask_flat * income).reshape(height, width))
    residual = linear_state - innovation
    residual_surface = mask_flat * residual[0, 0].reshape(-1)
    outgoing = live_weight * jnp.take(residual_surface, placed)
    chosen = pulled
    segment_ids = chosen + (jnp.arange(1 * lax.axis_size("lat"), dtype=jnp.int32) * cells)[:, None]
    summed = jax.ops.segment_sum(
        outgoing.reshape(-1), segment_ids.reshape(-1), num_segments=1 * lax.axis_size("lat") * cells
    )
    band_sums = lax.psum_scatter(
        summed.reshape(1 * lax.axis_size("lat"), cells), "lat", scatter_dimension=0, tiled=True
    )
    returned = partner_2(band_sums, "comp", 0)[0]
    adjoint_state = residual.at[0, 0].add((mask_flat * returned).reshape(height, width))
    adjoint_state = sweep(adjoint_state)
    gradient = adjoint_state + increment
    return (linear_state, gradient)


def solution(mesh):
    placed = (
        P("comp", None, "lat", "lon"),
        P("comp", None, "lat", "lon"),
        P("comp", None, "lat", "lon"),
        P("lat", "lon"),
        P("comp", "lat", "lon", None, None),
        P("comp", "lat", "lon", None, None),
        P("comp", "lat", "lon", None, None),
        P("comp", "lat", "lon", None),
    )
    return jax.shard_map(
        local,
        mesh=mesh,
        in_specs=placed,
        out_specs=(P("comp", None, "lat", "lon"), P("comp", None, "lat", "lon")),
        check_vma=False,
    )
```

profile of v0, /device:TPU:8, one launch (start us, length us, event | category | flops | bytes accessed | tf_op | source)
XLA Modules:
  0.0 1201.9 jit_solution(17627987960869966401)
XLA Ops:
  10.6 3.8 collective-permute-start.4
  16.1 3.8 collective-permute-start.5
  19.9 4.1 collective-permute-start.11
  31.3 3.6 collective-permute-start.8
  39.0 4.6 collective-permute-done.7
  49.3 3.7 collective-permute-done.3
  53.5 3.9 collective-permute-start.17
  66.3 3.6 collective-permute-done.13
  70.2 6.0 collective-permute-start.23
  85.1 3.6 collective-permute-done.19
  89.1 6.0 collective-permute-start.29
  103.9 3.6 collective-permute-done.25
  111.5 71.1 %all-gather.3.cloned.1.call-done = f32[32,1,8192]{2,1,0:T(1,128)} async-done(((f32[1,1,8192]{2,1,0:T(1,128)}), f32[32,1,8192]{2,1,0:T(1,128)}) %all-gather.3.cloned.1.call-update) | async-done | bytes 1048592 | tf_op jit(solution)/shard_map/all_gather | solution.py:99
  184.4 258.4 %gather_fusion.1 = f32[32768]{0:T(1024)S(1)} fusion(f32[32,8192]{1,0:T(8,128)S(1)} %bitcast.88, s32[32768]{0:T(1024)S(1)} %bitcast.89), kind=kCustom, calls=%fused_computation.1 | custom fusion | bytes 524288 | tf_op jit(solution)/shard_map/jit(take_along_axis)/gather | solution.py:98
  442.9 171.1 %scatter_custom_fusion = f32[8192]{0:T(1024)S(1)} fusion(s32[32768]{0:T(1024)S(1)} %bitcast.94, f32[32768]{0:T(1024)S(1)} %select_multiply_fusion.1, f32[]{:T(128)} %constant.98.clone.1), kind=kCustom, calls=%fused_computation.200 | custom fusion | flops 32768 | bytes 32772 | tf_op jit(solution)/shard_map/scatter-add | solution.py:101
  615.2 180.5 %gather_fusion = f32[32768]{0:T(1024)S(1)} fusion(f32[8192]{0:T(1024)S(1)} %mul.242, s32[32768]{0:T(1024)S(1)} %broadcast_clamp_fusion), kind=kCustom, calls=%fused_computation | custom fusion | bytes 393216 | tf_op jit(solution)/shard_map/jit(_take)/gather | solution.py:107
  795.8 171.6 %scatter_custom_fusion.1 = f32[262144]{0:T(1024)S(1)} fusion(s32[32768]{0:T(1024)} %bitcast.105, f32[32768]{0:T(1024)S(1)} %select_multiply_fusion, f32[]{:T(128)} %constant.98.clone.1), kind=kCustom, calls=%fused_computation.9 | custom fusion | flops 32768 | bytes 1049088 | tf_op jit(solution)/shard_map/scatter-add | solution.py:110
  969.8 145.8 %all-reduce.3.cloned.1.call-done = f32[32,8192]{1,0:T(8,128)} async-done(((f32[32,8192]{1,0:T(8,128)}), f32[32,8192]{1,0:T(8,128)}) %all-reduce.3.cloned.1.call-update) | async-done | bytes 1048592
  1121.4 4.9 collective-permute-start.37
  1138.1 6.0 collective-permute-start.43
  1152.7 3.6 collective-permute-done.39
  1156.7 6.0 collective-permute-start.49
  1171.5 3.6 collective-permute-done.45
  1175.5 6.2 collective-permute-start.55
  (210 shorter events, 107.6 us)
Async XLA Ops:
  7.2 175.4 %all-gather.3.cloned.1.call-start = ((), (), s32[]{:S(2)}) async-start(), calls=%async_computation | async-start | bytes 1081344 | tf_op jit(solution)/shard_map/all_gather | solution.py:99
  9.0 29.2 %collective-permute-start.6 = (f32[1,9,1,512]{3,2,1,0:T(1,128)S(1)}, f32[1,9,1,512]{3,2,1,0:T(1,128)S(1)}, u32[]{:S(2)}, u32[]{:S(2)}) collective-permute-start(f32[1,9,1,512]{3,2,1,0:T(1,128)S(1)} %get-tuple-element.37), channel_id=1, source_target_pairs={{0,1},{1,0},{2,3},{3,2},{4,5},{5,4},{6,7},{7,6},{8,9},{9,8},{10,11... | collective-permute-start | bytes 55304 | tf_op jit(solution)/shard_map/ppermute | solution.py:12
  10.6 38.5 %collective-permute-start.4 = (f32[1,9,1,512]{3,2,1,0:T(1,128)S(1)}, f32[1,9,1,512]{3,2,1,0:T(1,128)S(1)}, u32[]{:S(2)}, u32[]{:S(2)}) collective-permute-start(f32[1,9,1,512]{3,2,1,0:T(1,128)S(1)} %get-tuple-element.37), channel_id=1, source_target_pairs={{0,4},{4,8},{8,12},{12,16},{16,20},{20,24},{24,28},{28,32},{32,36}... | collective-permute-start | bytes 55304 | tf_op jit(solution)/shard_map/ppermute | solution.py:23
  15.4 10.5 collective-permute-start.9
  16.1 36.9 %collective-permute-start.5 = (f32[1,8,1,512]{3,2,1,0:T(1,128)S(1)}, f32[1,8,1,512]{3,2,1,0:T(1,128)S(1)}, u32[]{:S(2)}, u32[]{:S(2)}) collective-permute-start(f32[1,8,1,512]{3,2,1,0:T(1,128)S(1)} %get-tuple-element.67), channel_id=1, source_target_pairs={{0,4},{4,8},{8,12},{12,16},{16,20},{20,24},{24,28},{28,32},{32,36}... | collective-permute-start | bytes 49160 | tf_op jit(solution)/shard_map/ppermute | solution.py:23
  19.9 15.5 %collective-permute-start.11 = (f32[1,8,1,512]{3,2,1,0:T(1,128)S(1)}, f32[1,8,1,512]{3,2,1,0:T(1,128)S(1)}, u32[]{:S(2)}, u32[]{:S(2)}) collective-permute-start(f32[1,8,1,512]{3,2,1,0:T(1,128)S(1)} %get-tuple-element.66), channel_id=1, source_target_pairs={{4,0},{8,4},{12,8},{16,12},{20,16},{24,20},{28,24},{32,28},{36,32}... | collective-permute-start | bytes 49160 | tf_op jit(solution)/shard_map/ppermute | solution.py:25
  31.3 12.8 %collective-permute-start.8 = (f32[1,9,1,512]{3,2,1,0:T(1,128)S(1)}, f32[1,9,1,512]{3,2,1,0:T(1,128)S(1)}, u32[]{:S(2)}, u32[]{:S(2)}) collective-permute-start(f32[1,9,1,512]{3,2,1,0:T(1,128)S(1)} %get-tuple-element.36), channel_id=1, source_target_pairs={{4,0},{8,4},{12,8},{16,12},{20,16},{24,20},{28,24},{32,28},{36,32}... | collective-permute-start | bytes 55304 | tf_op jit(solution)/shard_map/ppermute | solution.py:25
  35.4 12.0 collective-permute-start
  53.5 11.3 collective-permute-start.17
  59.0 10.8 collective-permute-start.14
  70.2 13.4 %collective-permute-start.23 = (f32[1,8,1,512]{3,2,1,0:T(1,128)S(1)}, f32[1,8,1,512]{3,2,1,0:T(1,128)S(1)}, u32[]{:S(2)}, u32[]{:S(2)}) collective-permute-start(f32[1,8,1,512]{3,2,1,0:T(1,128)S(1)} %get-tuple-element.58), channel_id=1, source_target_pairs={{4,0},{8,4},{12,8},{16,12},{20,16},{24,20},{28,24},{32,28},{36,32}... | collective-permute-start | bytes 49160 | tf_op jit(solution)/shard_map/ppermute | solution.py:25
  77.9 10.7 collective-permute-start.20
  89.1 13.4 %collective-permute-start.29 = (f32[1,8,1,512]{3,2,1,0:T(1,128)S(1)}, f32[1,8,1,512]{3,2,1,0:T(1,128)S(1)}, u32[]{:S(2)}, u32[]{:S(2)}) collective-permute-start(f32[1,8,1,512]{3,2,1,0:T(1,128)S(1)} %get-tuple-element.54), channel_id=1, source_target_pairs={{4,0},{8,4},{12,8},{16,12},{20,16},{24,20},{28,24},{32,28},{36,32}... | collective-permute-start | bytes 49160 | tf_op jit(solution)/shard_map/ppermute | solution.py:25
  96.8 10.7 collective-permute-start.26
  109.8 1005.8 %all-reduce.3.cloned.1.call-start = ((), (), s32[]{:S(2)}) async-start(), calls=%async_computation.1 | async-start | bytes 2097152
  1121.4 12.5 %collective-permute-start.37 = (f32[1,8,1,512]{3,2,1,0:T(1,128)S(1)}, f32[1,8,1,512]{3,2,1,0:T(1,128)S(1)}, u32[]{:S(2)}, u32[]{:S(2)}) collective-permute-start(f32[1,8,1,512]{3,2,1,0:T(1,128)S(1)} %get-tuple-element.50), channel_id=1, source_target_pairs={{4,0},{8,4},{12,8},{16,12},{20,16},{24,20},{28,24},{32,28},{36,32}... | collective-permute-start | bytes 49160 | tf_op jit(solution)/shard_map/ppermute | solution.py:25
  1126.4 7.1 collective-permute-start.36
  1129.2 8.3 collective-permute-start.34
  1138.1 13.1 %collective-permute-start.43 = (f32[1,8,1,512]{3,2,1,0:T(1,128)S(1)}, f32[1,8,1,512]{3,2,1,0:T(1,128)S(1)}, u32[]{:S(2)}, u32[]{:S(2)}) collective-permute-start(f32[1,8,1,512]{3,2,1,0:T(1,128)S(1)} %get-tuple-element.46), channel_id=1, source_target_pairs={{4,0},{8,4},{12,8},{16,12},{20,16},{24,20},{28,24},{32,28},{36,32}... | collective-permute-start | bytes 49160 | tf_op jit(solution)/shard_map/ppermute | solution.py:25
  1145.6 10.7 collective-permute-start.40
  1156.7 13.4 %collective-permute-start.49 = (f32[1,8,1,512]{3,2,1,0:T(1,128)S(1)}, f32[1,8,1,512]{3,2,1,0:T(1,128)S(1)}, u32[]{:S(2)}, u32[]{:S(2)}) collective-permute-start(f32[1,8,1,512]{3,2,1,0:T(1,128)S(1)} %get-tuple-element.42), channel_id=1, source_target_pairs={{4,0},{8,4},{12,8},{16,12},{20,16},{24,20},{28,24},{32,28},{36,32}... | collective-permute-start | bytes 49160 | tf_op jit(solution)/shard_map/ppermute | solution.py:25
  1164.4 10.7 collective-permute-start.46
  1175.5 13.5 %collective-permute-start.55 = (f32[1,8,1,512]{3,2,1,0:T(1,128)S(1)}, f32[1,8,1,512]{3,2,1,0:T(1,128)S(1)}, u32[]{:S(2)}, u32[]{:S(2)}) collective-permute-start(f32[1,8,1,512]{3,2,1,0:T(1,128)S(1)} %get-tuple-element.38), channel_id=1, source_target_pairs={{4,0},{8,4},{12,8},{16,12},{20,16},{24,20},{28,24},{32,28},{36,32}... | collective-permute-start | bytes 49160 | tf_op jit(solution)/shard_map/ppermute | solution.py:25
  1183.2 10.9 collective-permute-start.52
  (44 other events, 574.8 us)
Sparse Core Ops, SparseCore 0:
  109.9 72.6 all-gather.2
  968.7 146.8 all-reduce.2
where the time goes:
time: 1200 us
  local copies, waits for them, and re-layouts  453 us (38%)
  other arithmetic  352 us (29%)
  waiting for transfers between devices  265 us (22%)
  starting transfers between devices  117 us (10%)
  between operations  15.1 us (1%)
    gather x1, local copies, waits for them, and re-layouts, local(): jnp.take_along_axis(lax.all_gather(other_surface, 'lat', axis=0, tiled=Tr...  258 us
    gather x1, local copies, waits for them, and re-layouts, local(): outgoing = live_weight * jnp.take(residual_surface, placed)  181 us
    scatter-add x1, other arithmetic, local(): jax.ops.segment_sum(outgoing.reshape(-1), segment_ids.reshape(-1), num_se...  172 us
    scatter-add x1, other arithmetic, local(): jax.ops.segment_sum((live_weight * values).reshape(-1), placed.reshape(-1...  171 us
    unnamed x3, waiting for transfers between devices  146 us
    ppermute x18, starting transfers between devices, extended(): lax.ppermute(head, axis, [((i + 1) % count, i) for i in range(ends)])  74 us
    all_gather x1, waiting for transfers between devices, local(): lax.all_gather(other_surface, 'lat', axis=0, tiled=True)  71.1 us
    ppermute x18, waiting for transfers between devices, extended(): lax.ppermute(tail, axis, [(i, (i + 1) % count) for i in range(ends)])  28.6 us
  transfers between devices with their start and end apart: 58, of which 22 were waited for; matrix products, arithmetic and copies ran while one was open for 1% of the time, Pallas kernels for 0%

commit v1 on v0

--- a/solution.py
+++ b/solution.py
@@ -95,9 +95,13 @@
     surface = mask_flat * state[0, 0].reshape(-1)
     other_surface = partner_2(surface[None, :], "comp", 0)
     chosen = pulled
-    values = jnp.take_along_axis(
-        lax.all_gather(other_surface, "lat", axis=0, tiled=True), chosen, axis=1
-    )
+
+    def packet_obtain(t0):
+        carry = jnp.stack([t0 for _ in range(jax.lax.axis_size("lat"))], axis=0)
+        heard = jax.lax.all_to_all(carry, split_axis=0, concat_axis=0, axis_name="lat")
+        return jnp.concatenate(heard, axis=0)
+
+    values = jnp.take_along_axis(packet_obtain(other_surface), chosen, axis=1)
     income = jax.ops.segment_sum(
         (live_weight * values).reshape(-1), placed.reshape(-1), num_segments=cells
     )

time: 1200 us -> 1170 us (0.975)
  waiting for transfers between devices: 265 us -> 213 us
    all_gather x1 -> x0, waiting for transfers between devices: 71.1 us -> none  [local(): lax.all_gather(other_surface, 'lat', axis=0, tiled=True)]
    all_to_all x0 -> x1, waiting for transfers between devices: none -> 21 us  [packet_obtain(): jax.lax.all_to_all(carry, split_axis=0, concat_axis=0, axis_name='lat')]
    unnamed x3 -> x2, waiting for transfers between devices: 146 us -> 144 us
where the time goes in v1:
time: 1170 us; the launch traced here: 1160 us
  local copies, waits for them, and re-layouts  457 us (39%)
  other arithmetic  352 us (30%)
  waiting for transfers between devices  213 us (18%)
  starting transfers between devices  126 us (11%)
  between operations  15.4 us (1%)
    gather x1, local copies, waits for them, and re-layouts, local(): values = jnp.take_along_axis(packet_obtain(other_surface), chosen, axis=1)  258 us
    gather x1, local copies, waits for them, and re-layouts, local(): outgoing = live_weight * jnp.take(residual_surface, placed)  181 us
    scatter-add x1, other arithmetic, local(): jax.ops.segment_sum(outgoing.reshape(-1), segment_ids.reshape(-1), num_se...  172 us
    scatter-add x1, other arithmetic, local(): jax.ops.segment_sum((live_weight * values).reshape(-1), placed.reshape(-1...  171 us
    unnamed x2, waiting for transfers between devices  144 us
    ppermute x18, starting transfers between devices, extended(): lax.ppermute(head, axis, [((i + 1) % count, i) for i in range(ends)])  74 us
    ppermute x18, waiting for transfers between devices, extended(): lax.ppermute(tail, axis, [(i, (i + 1) % count) for i in range(ends)])  29.1 us
  transfers between devices with their start and end apart: 58, of which 22 were waited for; matrix products, arithmetic and copies ran while one was open for 1% of the time, Pallas kernels for 0%

profile of v1, /device:TPU:8, one launch (start us, length us, event | category | flops | bytes accessed | tf_op | source)
XLA Modules:
  0.0 1162.8 jit_solution(1563135053611998159)
XLA Ops:
  10.6 3.8 collective-permute-start.4
  16.0 3.8 collective-permute-start.5
  19.9 4.1 collective-permute-start.11
  31.3 3.6 collective-permute-start.8
  39.0 4.6 collective-permute-done.7
  49.2 3.7 collective-permute-done.3
  53.5 3.9 collective-permute-start.17
  66.2 3.6 collective-permute-done.13
  70.2 6.0 collective-permute-start.23
  85.0 4.1 collective-permute-done.19
  89.6 5.9 collective-permute-start.29
  98.7 3.6 collective-permute-start.24
  104.3 3.6 collective-permute-done.25
  111.4 8.9 all-to-all-start
  125.8 21.0 %all-to-all-done = f32[32,1,8192]{2,1,0:T(1,128)S(1)} async-done(((f32[32,1,8192]{2,1,0:T(1,128)}), f32[32,1,8192]{2,1,0:T(1,128)S(1)}, u32[]{:S(2)}, u32[]{:S(2)}) %all-to-all-start) | async-done | bytes 1048608 | tf_op jit(solution)/shard_map/all_to_all | solution.py:101
  147.4 258.4 %gather_fusion.1 = f32[32768]{0:T(1024)S(1)} fusion(f32[32,8192]{1,0:T(8,128)S(1)} %bitcast.88, s32[32768]{0:T(1024)S(1)} %bitcast.89), kind=kCustom, calls=%fused_computation.1 | custom fusion | bytes 524288 | tf_op jit(solution)/shard_map/jit(take_along_axis)/gather | solution.py:104
  406.0 171.1 %scatter_custom_fusion = f32[8192]{0:T(1024)S(1)} fusion(s32[32768]{0:T(1024)S(1)} %bitcast.94, f32[32768]{0:T(1024)S(1)} %select_multiply_fusion.1, f32[]{:T(128)} %constant.98.clone.1), kind=kCustom, calls=%fused_computation.200 | custom fusion | flops 32768 | bytes 32772 | tf_op jit(solution)/shard_map/scatter-add | solution.py:105
  578.2 180.5 %gather_fusion = f32[32768]{0:T(1024)S(1)} fusion(f32[8192]{0:T(1024)S(1)} %mul.242, s32[32768]{0:T(1024)S(1)} %copy-done.10), kind=kCustom, calls=%fused_computation | custom fusion | bytes 393216 | tf_op jit(solution)/shard_map/jit(_take)/gather | solution.py:111
  758.9 171.6 %scatter_custom_fusion.1 = f32[262144]{0:T(1024)S(1)} fusion(s32[32768]{0:T(1024)} %bitcast.105, f32[32768]{0:T(1024)S(1)} %select_multiply_fusion, f32[]{:T(128)} %constant.98.clone.1), kind=kCustom, calls=%fused_computation.9 | custom fusion | flops 32768 | bytes 1049088 | tf_op jit(solution)/shard_map/scatter-add | solution.py:114
  932.9 143.5 %all-reduce.3.cloned.1.call-done = f32[32,8192]{1,0:T(8,128)} async-done(((f32[32,8192]{1,0:T(8,128)}), f32[32,8192]{1,0:T(8,128)}) %all-reduce.3.cloned.1.call-update) | async-done | bytes 1048592
  1082.2 4.9 collective-permute-start.37
  1098.9 6.0 collective-permute-start.43
  1117.5 6.0 collective-permute-start.49
  1136.3 6.2 collective-permute-start.55
  (226 shorter events, 115.0 us)
Async XLA Ops:
  9.0 29.2 %collective-permute-start.6 = (f32[1,9,1,512]{3,2,1,0:T(1,128)S(1)}, f32[1,9,1,512]{3,2,1,0:T(1,128)S(1)}, u32[]{:S(2)}, u32[]{:S(2)}) collective-permute-start(f32[1,9,1,512]{3,2,1,0:T(1,128)S(1)} %get-tuple-element.37), channel_id=1, source_target_pairs={{0,1},{1,0},{2,3},{3,2},{4,5},{5,4},{6,7},{7,6},{8,9},{9,8},{10,11... | collective-permute-start | bytes 55304 | tf_op jit(solution)/shard_map/ppermute | solution.py:12
  10.6 38.5 %collective-permute-start.4 = (f32[1,9,1,512]{3,2,1,0:T(1,128)S(1)}, f32[1,9,1,512]{3,2,1,0:T(1,128)S(1)}, u32[]{:S(2)}, u32[]{:S(2)}) collective-permute-start(f32[1,9,1,512]{3,2,1,0:T(1,128)S(1)} %get-tuple-element.37), channel_id=1, source_target_pairs={{0,4},{4,8},{8,12},{12,16},{16,20},{20,24},{24,28},{28,32},{32,36}... | collective-permute-start | bytes 55304 | tf_op jit(solution)/shard_map/ppermute | solution.py:23
  15.4 10.5 collective-permute-start.9
  16.0 36.9 %collective-permute-start.5 = (f32[1,8,1,512]{3,2,1,0:T(1,128)S(1)}, f32[1,8,1,512]{3,2,1,0:T(1,128)S(1)}, u32[]{:S(2)}, u32[]{:S(2)}) collective-permute-start(f32[1,8,1,512]{3,2,1,0:T(1,128)S(1)} %get-tuple-element.67), channel_id=1, source_target_pairs={{0,4},{4,8},{8,12},{12,16},{16,20},{20,24},{24,28},{28,32},{32,36}... | collective-permute-start | bytes 49160 | tf_op jit(solution)/shard_map/ppermute | solution.py:23
  19.9 15.5 %collective-permute-start.11 = (f32[1,8,1,512]{3,2,1,0:T(1,128)S(1)}, f32[1,8,1,512]{3,2,1,0:T(1,128)S(1)}, u32[]{:S(2)}, u32[]{:S(2)}) collective-permute-start(f32[1,8,1,512]{3,2,1,0:T(1,128)S(1)} %get-tuple-element.66), channel_id=1, source_target_pairs={{4,0},{8,4},{12,8},{16,12},{20,16},{24,20},{28,24},{32,28},{36,32}... | collective-permute-start | bytes 49160 | tf_op jit(solution)/shard_map/ppermute | solution.py:25
  31.3 12.8 %collective-permute-start.8 = (f32[1,9,1,512]{3,2,1,0:T(1,128)S(1)}, f32[1,9,1,512]{3,2,1,0:T(1,128)S(1)}, u32[]{:S(2)}, u32[]{:S(2)}) collective-permute-start(f32[1,9,1,512]{3,2,1,0:T(1,128)S(1)} %get-tuple-element.36), channel_id=1, source_target_pairs={{4,0},{8,4},{12,8},{16,12},{20,16},{24,20},{28,24},{32,28},{36,32}... | collective-permute-start | bytes 55304 | tf_op jit(solution)/shard_map/ppermute | solution.py:25
  35.4 12.0 %collective-permute-start = (f32[1,9,16,1]{3,2,1,0:T(8,128)S(1)}, f32[1,9,16,1]{3,2,1,0:T(8,128)S(1)}, u32[]{:S(2)}, u32[]{:S(2)}) collective-permute-start(f32[1,9,16,1]{3,2,1,0:T(8,128)S(1)} %get-tuple-element.35), channel_id=1, source_target_pairs={{1,0},{2,1},{3,2},{0,3},{5,4},{6,5},{7,6},{4,7},{9,8},{10,9},{11,1... | collective-permute-start | bytes 1736 | tf_op jit(solution)/shard_map/ppermute | solution.py:25
  53.5 11.3 collective-permute-start.17
  59.0 10.8 collective-permute-start.14
  70.2 13.8 %collective-permute-start.23 = (f32[1,8,1,512]{3,2,1,0:T(1,128)S(1)}, f32[1,8,1,512]{3,2,1,0:T(1,128)S(1)}, u32[]{:S(2)}, u32[]{:S(2)}) collective-permute-start(f32[1,8,1,512]{3,2,1,0:T(1,128)S(1)} %get-tuple-element.58), channel_id=1, source_target_pairs={{4,0},{8,4},{12,8},{16,12},{20,16},{24,20},{28,24},{32,28},{36,32}... | collective-permute-start | bytes 49160 | tf_op jit(solution)/shard_map/ppermute | solution.py:25
  76.2 7.3 collective-permute-start.22
  77.9 11.3 collective-permute-start.20
  89.6 13.2 %collective-permute-start.29 = (f32[1,8,1,512]{3,2,1,0:T(1,128)S(1)}, f32[1,8,1,512]{3,2,1,0:T(1,128)S(1)}, u32[]{:S(2)}, u32[]{:S(2)}) collective-permute-start(f32[1,8,1,512]{3,2,1,0:T(1,128)S(1)} %get-tuple-element.54), channel_id=1, source_target_pairs={{4,0},{8,4},{12,8},{16,12},{20,16},{24,20},{28,24},{32,28},{36,32}... | collective-permute-start | bytes 49160 | tf_op jit(solution)/shard_map/ppermute | solution.py:25
  96.8 11.1 collective-permute-start.26
  111.4 35.3 %all-to-all-start = ((f32[32,1,8192]{2,1,0:T(1,128)}), f32[32,1,8192]{2,1,0:T(1,128)S(1)}, u32[]{:S(2)}, u32[]{:S(2)}) async-start(f32[32,1,8192]{2,1,0:T(1,128)} %stack.2), calls=%async_computation | async-start | bytes 2097152 | tf_op jit(solution)/shard_map/all_to_all | solution.py:101
  120.3 956.1 %all-reduce.3.cloned.1.call-start = ((), (), s32[]{:S(2)}) async-start(), calls=%async_computation.1 | async-start | bytes 2097152
  1082.2 12.5 %collective-permute-start.37 = (f32[1,8,1,512]{3,2,1,0:T(1,128)S(1)}, f32[1,8,1,512]{3,2,1,0:T(1,128)S(1)}, u32[]{:S(2)}, u32[]{:S(2)}) collective-permute-start(f32[1,8,1,512]{3,2,1,0:T(1,128)S(1)} %get-tuple-element.50), channel_id=1, source_target_pairs={{4,0},{8,4},{12,8},{16,12},{20,16},{24,20},{28,24},{32,28},{36,32}... | collective-permute-start | bytes 49160 | tf_op jit(solution)/shard_map/ppermute | solution.py:25
  1090.2 8.0 collective-permute-start.34
  1098.9 13.1 %collective-permute-start.43 = (f32[1,8,1,512]{3,2,1,0:T(1,128)S(1)}, f32[1,8,1,512]{3,2,1,0:T(1,128)S(1)}, u32[]{:S(2)}, u32[]{:S(2)}) collective-permute-start(f32[1,8,1,512]{3,2,1,0:T(1,128)S(1)} %get-tuple-element.46), channel_id=1, source_target_pairs={{4,0},{8,4},{12,8},{16,12},{20,16},{24,20},{28,24},{32,28},{36,32}... | collective-permute-start | bytes 49160 | tf_op jit(solution)/shard_map/ppermute | solution.py:25
  1106.3 10.7 collective-permute-start.40
  1117.5 13.4 %collective-permute-start.49 = (f32[1,8,1,512]{3,2,1,0:T(1,128)S(1)}, f32[1,8,1,512]{3,2,1,0:T(1,128)S(1)}, u32[]{:S(2)}, u32[]{:S(2)}) collective-permute-start(f32[1,8,1,512]{3,2,1,0:T(1,128)S(1)} %get-tuple-element.42), channel_id=1, source_target_pairs={{4,0},{8,4},{12,8},{16,12},{20,16},{24,20},{28,24},{32,28},{36,32}... | collective-permute-start | bytes 49160 | tf_op jit(solution)/shard_map/ppermute | solution.py:25
  1125.1 10.7 collective-permute-start.46
  1136.3 13.5 %collective-permute-start.55 = (f32[1,8,1,512]{3,2,1,0:T(1,128)S(1)}, f32[1,8,1,512]{3,2,1,0:T(1,128)S(1)}, u32[]{:S(2)}, u32[]{:S(2)}) collective-permute-start(f32[1,8,1,512]{3,2,1,0:T(1,128)S(1)} %get-tuple-element.38), channel_id=1, source_target_pairs={{4,0},{8,4},{12,8},{16,12},{20,16},{24,20},{28,24},{32,28},{36,32}... | collective-permute-start | bytes 49160 | tf_op jit(solution)/shard_map/ppermute | solution.py:25
  1143.9 10.9 collective-permute-start.52
  (52 other events, 2842.4 us)
Sparse Core Ops, SparseCore 0:
  931.8 144.5 all-reduce.2
